TPU v7x, 32 devices: a whole 2x2x4 slice. The times are simulated.
32 devices in a mesh: grp: 2 (over y), tm: 4 (over z), mod: 4 (over x, core).
Axes of the slice: x: 2, y: 2, z: 4, core: 2. Of those that a mesh axis runs over, the one named last changes fastest.
Arguments:
- phase: float32 [16, 512, 128], P(('grp', 'tm'), 'mod'), parts along dimension 0, may hold values from -4 to 4
- direction: float32 [16, 512, 128], P(('grp', 'tm'), 'mod'), parts along dimension 0, may hold values from -16 to 16
- pupil_mask: int32 [512, 128], replicated, may hold values 0 or 1
- mod_tilts: int32 [4], P('mod'), may hold values from -8 to 8
- wind_codes: int32 [1024, 128], P('grp'), parts along dimension 0, may hold values from 0 to 15
- noise_weight: float32 [16, 1024, 128], P(('grp', 'tm')), parts along dimension 0, may hold values from 0.075 to 0.75
Outputs:
- hess_vec: float32 [16, 512, 128], P(('grp', 'tm'), 'mod'), parts along dimension 0
- curvature: float32 [2], P('grp'), parts along dimension 0
There are 2 independent parts, one for each index of `grp`. A program takes and returns all parts, laid end to end along the dimension named above; an argument that names none is the same for every part. Nothing has to cross between parts.
All inputs are finite; a program needn't handle non-finite values.
Results may differ from a plain program's by a relative error of at most 0.0003.
Values sent between devices are 32-bit elements; how exact they have to be, the bound alone decides.
A program may use at most 64 MiB of HBM per device.

v0:
```python
import jax
import jax.numpy as jnp
from jax import lax
from jax.sharding import PartitionSpec as P

HIGHEST = lax.Precision.HIGHEST


def with_halo(cells, sides, width):
    for axis, dim in sides:
        count = lax.axis_size(axis)
        ends = count - 1
        head = lax.slice_in_dim(cells, 0, width, axis=dim)
        tail = lax.slice_in_dim(cells, cells.shape[dim] - width, cells.shape[dim], axis=dim)
        cells = jnp.concatenate(
            [
                lax.ppermute(tail, axis, [(i, (i + 1) % count) for i in range(ends)]),
                cells,
                lax.ppermute(head, axis, [((i + 1) % count, i) for i in range(ends)]),
            ],
            axis=dim,
        )
    return cells


def square_table(count, orient):
    index_range = jnp.arange(count, dtype=jnp.int32)
    turn_counts = index_range[:, None] * index_range[None, :] % count
    angles = orient * 2.0 * jnp.pi / count * turn_counts.astype(jnp.float32)
    return (jnp.cos(angles), jnp.sin(angles))


def complex_mix(form, table_real, table_imag, field_real, field_imag):
    real_real = jnp.einsum(form, table_real, field_real, precision=HIGHEST)
    imag_imag = jnp.einsum(form, table_imag, field_imag, precision=HIGHEST)
    real_imag = jnp.einsum(form, table_real, field_imag, precision=HIGHEST)
    imag_real = jnp.einsum(form, table_imag, field_real, precision=HIGHEST)
    return (real_real - imag_imag, real_imag + imag_real)


def transform(field_real, field_imag, orient):
    batch_size, length, row_count = field_real.shape
    outer_size = 32
    inner_size = length // outer_size
    first_real, first_imag = square_table(outer_size, orient)
    second_real, second_imag = square_table(inner_size, orient)
    turn_counts = (
        jnp.arange(outer_size, dtype=jnp.int32)[:, None]
        * jnp.arange(inner_size, dtype=jnp.int32)[None, :]
        % length
    )
    angles = orient * 2.0 * jnp.pi / length * turn_counts.astype(jnp.float32)
    twist_real = jnp.cos(angles)[None, :, :, None]
    twist_imag = jnp.sin(angles)[None, :, :, None]
    shaped_real = field_real.reshape(batch_size, outer_size, inner_size, row_count)
    shaped_imag = field_imag.reshape(batch_size, outer_size, inner_size, row_count)
    section_real, section_imag = complex_mix(
        "kn,bnmr->bkmr", first_real, first_imag, shaped_real, shaped_imag
    )
    turned_real = section_real * twist_real - section_imag * twist_imag
    turned_imag = section_real * twist_imag + section_imag * twist_real
    final_real, final_imag = complex_mix(
        "dm,bkmr->bdkr", second_real, second_imag, turned_real, turned_imag
    )
    return (
        final_real.reshape(batch_size, length, row_count),
        final_imag.reshape(batch_size, length, row_count),
    )


def roof_mask(length, shift_bins):
    freq_index = jnp.arange(length, dtype=jnp.int32)
    signed_freq = jnp.where(freq_index < length // 2, freq_index, freq_index - length)
    turn_counts = shift_bins * jnp.abs(signed_freq) % length
    angles = -2.0 * jnp.pi / length * turn_counts.astype(jnp.float32)
    return (jnp.cos(angles), jnp.sin(angles))


def pyramid(field_real, field_imag, gain_real, gain_imag):
    spectrum_real, spectrum_imag = transform(field_real, field_imag, -1.0)
    column_real = gain_real[None, :, None]
    column_imag = gain_imag[None, :, None]
    masked_real = spectrum_real * column_real - spectrum_imag * column_imag
    masked_imag = spectrum_real * column_imag + spectrum_imag * column_real
    back_real, back_imag = transform(masked_real, masked_imag, 1.0)
    inverse_length = 1.0 / field_real.shape[1]
    return (back_real * inverse_length, back_imag * inverse_length)


def row_ahead(field):
    return jnp.pad(field[:, :, 1:], ((0, 0), (0, 0), (0, 1)))


def row_behind(field):
    return jnp.pad(field[:, :, :-1], ((0, 0), (0, 0), (1, 0)))


def flow_terms(extended, frac_x, frac_r, first_frame, total_frames, first_pixel):
    frames_ext, width_ext, row_count = extended.shape
    frames_dev = frames_ext - 2
    near_x = jnp.pad(frac_x, ((1, 0), (0, 0)))
    near_r = jnp.pad(frac_r, ((1, 0), (0, 0)))
    stay_stay = (1.0 - near_x) * (1.0 - near_r)
    ahead_stay = near_x * (1.0 - near_r)
    stay_ahead = (1.0 - near_x) * near_r
    ahead_ahead = near_x * near_r
    base_cells = extended[:, :-1, :]
    ahead_cells = extended[:, 1:, :]
    moved = (
        stay_stay * base_cells
        + ahead_stay * ahead_cells
        + stay_ahead * row_ahead(base_cells)
        + ahead_ahead * row_ahead(ahead_cells)
    )
    flow = extended[1:, :-1, :] - moved[:-1]
    frame_ids = first_frame - 1 + lax.broadcasted_iota(jnp.int32, flow.shape, 0)
    pixel_ids = first_pixel - 1 + lax.broadcasted_iota(jnp.int32, flow.shape, 1)
    valid = (frame_ids >= 0) & (frame_ids <= total_frames - 2) & (pixel_ids >= 0)
    flow = jnp.where(valid, flow, 0.0)
    spread = (
        (stay_stay * flow)[:, 1:]
        + (ahead_stay * flow)[:, :-1]
        + row_behind((stay_ahead * flow)[:, 1:] + (ahead_ahead * flow)[:, :-1])
    )
    prior = flow[:frames_dev, 1:] - spread[1:]
    return (prior, flow[1:, 1:])


def forward_pass(full_phase, full_direction, tilts, amplitude, gain_real, gain_imag):
    frames_dev, pupil_width, row_count = full_phase.shape
    line_length = 2 * pupil_width
    quarter = pupil_width // 2
    local_points = tilts.shape[0]
    positions = quarter + jnp.arange(pupil_width, dtype=jnp.int32)
    tilt_turns = tilts[:, None] * positions[None, :] % line_length
    tilt_angles = 2.0 * jnp.pi / line_length * tilt_turns.astype(jnp.float32)
    angles = full_phase[None] + tilt_angles[:, None, :, None]
    field_real = amplitude * jnp.cos(angles)
    field_imag = amplitude * jnp.sin(angles)
    margins = ((0, 0), (quarter, quarter), (0, 0))
    line_batch = local_points * frames_dev

    def padded_lines(field):
        return jnp.pad(field.reshape(line_batch, pupil_width, row_count), margins)

    image_real, image_imag = pyramid(
        padded_lines(field_real), padded_lines(field_imag), gain_real, gain_imag
    )
    push_real, push_imag = pyramid(
        padded_lines(-field_imag * full_direction),
        padded_lines(field_real * full_direction),
        gain_real,
        gain_imag,
    )
    signal_terms = (2.0 * (image_real * push_real + image_imag * push_imag)).reshape(
        local_points, frames_dev, line_length, row_count
    )
    return (field_real, field_imag, image_real, image_imag, jnp.sum(signal_terms, axis=0))


def backward_pass(
    field_real, field_imag, image_real, image_imag, weighted_full, gain_real, gain_imag
):
    local_points, frames_dev, pupil_width, row_count = field_real.shape
    line_length = 2 * pupil_width
    quarter = pupil_width // 2
    line_batch = local_points * frames_dev
    image_shaped_real = image_real.reshape(local_points, frames_dev, line_length, row_count)
    image_shaped_imag = image_imag.reshape(local_points, frames_dev, line_length, row_count)
    source_real = (weighted_full[None] * image_shaped_real).reshape(
        line_batch, line_length, row_count
    )
    source_imag = (weighted_full[None] * image_shaped_imag).reshape(
        line_batch, line_length, row_count
    )
    back_real, back_imag = pyramid(source_real, source_imag, gain_real, -gain_imag)
    back_real = back_real[:, quarter : quarter + pupil_width].reshape(
        local_points, frames_dev, pupil_width, row_count
    )
    back_imag = back_imag[:, quarter : quarter + pupil_width].reshape(
        local_points, frames_dev, pupil_width, row_count
    )
    return -2.0 * jnp.sum(field_imag * back_real - field_real * back_imag, axis=0)


def per_device(phase, direction, pupil_mask, mod_tilts, wind_codes, noise_weight):
    frames_dev, shard_width, row_count = phase.shape
    mod_count = lax.axis_size("mod")
    pupil_width = shard_width * mod_count
    line_length = 2 * pupil_width
    quarter = pupil_width // 2
    mod_index = lax.axis_index("mod")
    first_frame = lax.axis_index("tm") * frames_dev
    total_frames = frames_dev * lax.axis_size("tm")
    first_pixel = mod_index * shard_width
    frac_x = ((wind_codes % 4).astype(jnp.float32) + 0.5) / 4.0
    frac_r = ((wind_codes // 4).astype(jnp.float32) + 0.5) / 4.0
    gain_real, gain_imag = roof_mask(line_length, quarter)
    rimmed = with_halo(direction, (("tm", 0),), 1)
    full_phase, full_rim = (
        lax.all_gather(phase, "mod", axis=1, tiled=True),
        lax.all_gather(rimmed, "mod", axis=1, tiled=True),
    )
    full_direction = full_rim[1:-1]
    extended = jnp.pad(full_rim, ((0, 0), (1, 1), (0, 0)))
    prior_lines, flow_lines = flow_terms(extended, frac_x, frac_r, first_frame, total_frames, 0)
    prior = lax.dynamic_slice_in_dim(prior_lines, first_pixel, shard_width, 1)
    amplitude = pupil_mask.astype(jnp.float32)
    field_real, field_imag, image_real, image_imag, signal_local = forward_pass(
        full_phase, full_direction, mod_tilts, amplitude, gain_real, gain_imag
    )
    signal_full = lax.psum(signal_local, "mod")
    weighted_used = noise_weight * signal_full
    grad_lines = backward_pass(
        field_real, field_imag, image_real, image_imag, weighted_used, gain_real, gain_imag
    )
    grad_own = lax.psum_scatter(grad_lines, "mod", scatter_dimension=1, tiled=True)
    hess_vec = grad_own + prior
    curvature_total = lax.psum(jnp.sum(direction * hess_vec), ("tm", "mod"))
    entry_count = float(total_frames * pupil_width * row_count)
    curvature = (curvature_total / entry_count).reshape(1)
    return (hess_vec, curvature)


def solution(mesh):
    return jax.shard_map(
        per_device,
        mesh=mesh,
        in_specs=(
            P(("grp", "tm"), "mod", None),
            P(("grp", "tm"), "mod", None),
            P(),
            P("mod"),
            P("grp", None),
            P(("grp", "tm"), None, None),
        ),
        out_specs=(P(("grp", "tm"), "mod", None), P("grp")),
        check_vma=False,
    )
```

profile of v0, /device:TPU:0, one launch (start us, length us, event | category | flops | bytes accessed | tf_op | source)
XLA Modules:
  0.0 235.1 jit_solution(14579527725214481166)
XLA Ops:
  8.1 5.0 %collective-permute-start = (f32[1,128,128]{2,1,0:T(8,128)S(1)}, f32[1,128,128]{2,1,0:T(8,128)S(1)}, u32[]{:S(2)}, u32[]{:S(2)}) collective-permute-start(f32[1,128,128]{2,1,0:T(8,128)S(1)} %get-tuple-element.39), channel_id=1, source_target_pairs={{0,4},{4,8},{8,12},{1,5},{5,9},{9,13},{2,6},{6,10},{10,14},{3,7},{... | collective-permute-start | bytes 196616 | tf_op jit(solution)/shard_map/ppermute | solution.py:17
  16.0 3.2 %collective-permute-done.1 = f32[1,128,128]{2,1,0:T(8,128)S(1)} collective-permute-done((f32[1,128,128]{2,1,0:T(8,128)S(1)}, f32[1,128,128]{2,1,0:T(8,128)S(1)}, u32[]{:S(2)}, u32[]{:S(2)}) %collective-permute-start.1) | collective-permute-done | bytes 65568 | tf_op jit(solution)/shard_map/ppermute | solution.py:19
  26.2 9.5 %all_gather.6 = f32[2,512,128]{2,1,0:T(8,128)S(1)} all-gather(f32[2,128,128]{2,1,0:T(8,128)S(1)} %copy-done.19), channel_id=1, replica_groups=mesh['grp'=2,'tm'=4,'mod'=4] {'mod'}, dimensions={1}, use_global_device_ids=true | all-gather | bytes 655360 | tf_op jit(solution)/shard_map/all_gather | solution.py:201
  35.7 4.0 %all-gather.2.cloned.1.call-done = f32[4,512,128]{2,1,0:T(8,128)} async-done(((f32[4,128,128]{2,1,0:T(8,128)}), f32[4,512,128]{2,1,0:T(8,128)}) %all-gather.2.cloned.1.call-update) | async-done | bytes 1048592 | tf_op jit(solution)/shard_map/all_gather | solution.py:202
  39.6 4.1 %negate_multiply_fusion = (f32[2,512,128]{2,1,0:T(8,128)S(1)}, f32[2,512,128]{2,1,0:T(8,128)S(1)}, f32[2,512,128]{2,1,0:T(8,128)S(1)}, f32[2,512,128]{2,1,0:T(8,128)S(1)}) fusion(f32[4,512,128]{2,1,0:T(8,128)} %all-gather.2.cloned.1.call-done, f32[2,512,128]{2,1,0:T(8,128)S(1)} %all_gather.6, f32[512]{0:T(512)S(1)} %fusion.179, ...), kind=kLoop, calls=%fused_computation.154 | loop fusion | flops 786432 | bytes 3409920 | tf_op jit(solution)/shard_map/mul | solution.py:150
  47.3 1.8 fusion.28
  49.1 1.8 fusion.29
  54.5 2.0 fusion.21
  56.5 2.2 multiply_subtract_fusion.5
  63.8 1.8 fusion.26
  68.2 1.9 fusion.60
  71.8 1.7 fusion.19
  73.6 1.7 fusion.18
  82.3 1.8 multiply_subtract_fusion.3
  87.5 1.8 fusion.15
  93.3 1.9 fusion.13
  95.8 1.8 fusion.11
  98.2 1.8 fusion.23
  105.3 2.0 pad_slice_fusion.1
  107.2 30.4 %all-reduce.12.cloned.1.call-done = f32[2,1024,128]{2,1,0:T(8,128)} async-done(((f32[2,1024,128]{2,1,0:T(8,128)}), f32[2,1024,128]{2,1,0:T(8,128)}) %all-reduce.12.cloned.1.call-update) | async-done | bytes 1048592 | tf_op jit(solution)/shard_map/psum | solution.py:212
  137.7 1.8 bitcast_multiply_fusion.3
  142.9 1.8 fusion.9
  144.7 2.1 multiply_subtract_fusion.2
  150.2 2.1 fusion.7
  152.4 1.8 fusion.6
  161.3 1.9 fusion.32
  163.2 1.7 fusion.3
  165.5 1.7 fusion.1
  170.2 2.1 fusion.87
  173.5 18.2 %reduce-scatter.2.cloned.1.call-done = f32[2,128,128]{2,1,0:T(8,128)} async-done(((f32[2,512,128]{2,1,0:T(8,128)}), f32[2,128,128]{2,1,0:T(8,128)}) %reduce-scatter.2.cloned.1.call-update) | async-done | bytes 131088 | tf_op jit(solution)/shard_map/reduce_scatter | solution.py:217
  191.7 2.3 multiply_reduce_fusion
  194.0 32.7 %psum.15 = f32[]{:T(128)} all-reduce(f32[]{:T(128)} %get-tuple-element.2), channel_id=1, replica_groups=mesh['grp'=2,'tm'=4,'mod'=4] {'tm','mod'}, use_global_device_ids=true, to_apply=%region_3.4 | all-reduce | flops 1 | bytes 8 | tf_op jit(solution)/shard_map/psum | solution.py:219
  (119 shorter events, 66.2 us)
Async XLA Ops:
  7.2 15.0 %copy-start.13 = (s32[512,128]{1,0:T(8,128)S(1)}, s32[512,128]{1,0:T(8,128)}, u32[]{:S(2)}) copy-start(s32[512,128]{1,0:T(8,128)} %param.10) | copy-start | bytes 786436
  7.2 32.5 %all-gather.2.cloned.1.call-start = ((), (), s32[]{:S(2)}) async-start(), calls=%async_computation.1 | async-start | bytes 1310720 | tf_op jit(solution)/shard_map/all_gather | solution.py:202
  8.1 7.9 %collective-permute-start = (f32[1,128,128]{2,1,0:T(8,128)S(1)}, f32[1,128,128]{2,1,0:T(8,128)S(1)}, u32[]{:S(2)}, u32[]{:S(2)}) collective-permute-start(f32[1,128,128]{2,1,0:T(8,128)S(1)} %get-tuple-element.39), channel_id=1, source_target_pairs={{0,4},{4,8},{8,12},{1,5},{5,9},{9,13},{2,6},{6,10},{10,14},{3,7},{... | collective-permute-start | bytes 196616 | tf_op jit(solution)/shard_map/ppermute | solution.py:17
  13.1 6.2 %collective-permute-start.1 = (f32[1,128,128]{2,1,0:T(8,128)S(1)}, f32[1,128,128]{2,1,0:T(8,128)S(1)}, u32[]{:S(2)}, u32[]{:S(2)}) collective-permute-start(f32[1,128,128]{2,1,0:T(8,128)S(1)} %get-tuple-element.40), channel_id=1, source_target_pairs={{4,0},{8,4},{12,8},{5,1},{9,5},{13,9},{6,2},{10,6},{14,10},{7,3},{... | collective-permute-start | bytes 196616 | tf_op jit(solution)/shard_map/ppermute | solution.py:19
  20.9 116.8 %all-reduce.12.cloned.1.call-start = ((), (), s32[]{:S(2)}) async-start(), calls=%async_computation.2 | async-start | bytes 2097152 | tf_op jit(solution)/shard_map/psum | solution.py:212
  21.1 35.3 %copy-start.15 = (f32[32,32]{0,1:T(8,128)}, f32[32,32]{0,1:T(8,128)S(1)}, u32[]{:S(2)}) copy-start(f32[32,32]{0,1:T(8,128)S(1)} %copy.45) | copy-start | bytes 12292
  21.3 35.2 %copy-start.17 = (f32[32,32]{0,1:T(8,128)}, f32[32,32]{0,1:T(8,128)S(1)}, u32[]{:S(2)}) copy-start(f32[32,32]{0,1:T(8,128)S(1)} %copy.48) | copy-start | bytes 12292
  22.5 0.7 copy-start.7
  22.5 1.5 copy-start.8
  22.5 13.1 %copy-start.9 = (f32[513,128]{1,0:T(8,128)}, f32[513,128]{1,0:T(8,128)S(1)}, u32[]{:S(2)}) copy-start(f32[513,128]{1,0:T(8,128)S(1)} %get-tuple-element.36) | copy-start | bytes 787972
  22.6 3.7 %copy-start.19 = (f32[2,128,128]{2,1,0:T(8,128)S(1)}, f32[2,128,128]{2,1,0:T(8,128)}, u32[]{:S(2)}) copy-start(f32[2,128,128]{2,1,0:T(8,128)} %param.6) | copy-start | bytes 393220
  43.7 1.8 copy-start.1
  43.7 1.8 copy-start.3
  101.9 1.9 copy-start
  101.9 89.8 %reduce-scatter.2.cloned.1.call-start = ((), (), s32[]{:S(2)}) async-start(), calls=%async_computation.3 | async-start | bytes 655360 | tf_op jit(solution)/shard_map/reduce_scatter | solution.py:217
  142.9 1.8 copy-start.16
  142.9 1.8 copy-start.18
  167.3 1.0 copy-start.2
  167.3 1.2 copy-start.4
  168.5 1.4 copy-start.5
  168.5 1.7 copy-start.6
  172.4 1.0 copy-start.11
  172.4 1.0 copy-start.12
  173.4 18.3 %copy-start.10 = (f32[2,128,128]{2,1,0:T(8,128)S(1)}, f32[2,128,128]{2,1,0:T(8,128)}, u32[]{:S(2)}) copy-start(f32[2,128,128]{2,1,0:T(8,128)} %param.7) | copy-start | bytes 393220
  173.4 18.3 %copy-start.14 = (f32[128,128]{1,0:T(8,128)S(1)}, f32[128,128]{1,0:T(8,128)}, u32[]{:S(2)}) copy-start(f32[128,128]{1,0:T(8,128)} %get-tuple-element.46) | copy-start | bytes 196612
Sparse Core Ops, SparseCore 0:
  21.0 18.5 all-gather.1
  102.0 35.5 all-reduce.11
  169.5 22.1 reduce-scatter.1
where the time goes:
time: 238 us; the launch traced here: 235 us
  matrix products  80.7 us (34%)
  waiting for transfers between devices  55.8 us (23%)
  blocking collectives  42.1 us (18%)
  between operations  17.1 us (7%)
  local copies, waits for them, and re-layouts  16.5 us (7%)
  other arithmetic  16.2 us (7%)
  starting transfers between devices  6.66 us (3%)
    psum x1, blocking collectives, per_device(): curvature_total = lax.psum(jnp.sum(direction * hess_vec), ('tm', 'mod'))  32.7 us
    psum x1, waiting for transfers between devices, per_device(): signal_full = lax.psum(signal_local, 'mod')  30.4 us
    dot_general x12, matrix products, complex_mix(): imag_real = jnp.einsum(form, table_imag, field_real, precision=HIGHEST)  21.3 us
    dot_general x12, matrix products, complex_mix(): imag_imag = jnp.einsum(form, table_imag, field_imag, precision=HIGHEST)  20.6 us
    dot_general x12, matrix products, complex_mix(): real_real = jnp.einsum(form, table_real, field_real, precision=HIGHEST)  19.4 us
    dot_general x12, matrix products, complex_mix(): real_imag = jnp.einsum(form, table_real, field_imag, precision=HIGHEST)  19.4 us
    reduce_scatter x1, waiting for transfers between devices, per_device(): lax.psum_scatter(grad_lines, 'mod', scatter_dimension=1, tiled=True)  18.2 us
    all_gather x1, blocking collectives, per_device(): lax.all_gather(phase, 'mod', axis=1, tiled=True)  9.45 us
  transfers between devices with their start and end apart: 5, of which 4 were waited for; matrix products, arithmetic and copies ran while one was open for 5% of the time, Pallas kernels for 0%

commit v1 on v0

--- a/solution.py
+++ b/solution.py
@@ -1,6 +1,11 @@
+import functools
+
 import jax
 import jax.numpy as jnp
+import numpy as np
 from jax import lax
+from jax.experimental import pallas as pl
+from jax.experimental.pallas import tpu as pltpu
 from jax.sharding import PartitionSpec as P
 
 HIGHEST = lax.Precision.HIGHEST
@@ -222,9 +227,612 @@
     return (hess_vec, curvature)
 
 
+TILE = 16
+HALO = 8
+
+
+def coupling_tables(pupil_width, pieces):
+    per_piece = pupil_width // pieces
+    order = [
+        np.concatenate([pieces * np.arange(per_piece) + j for j in range(parity, pieces, 2)])
+        for parity in (0, 1)
+    ]
+    tables = []
+    for source in (0, 1):
+        gap = order[1 - source][:, None] - order[source][None, :]
+        exact = -1.0 / (pupil_width * np.sin(np.pi * gap / pupil_width))
+        high = exact.astype(jnp.bfloat16)
+        low = (exact - high.astype(np.float64)).astype(jnp.bfloat16)
+        tables.append(np.concatenate([high, high, low], axis=1))
+    return np.stack(tables)
+
+
+def cos_sin(angle):
+    turns = jnp.round(angle * np.float32(2.0 / np.pi))
+    rest = angle - turns * np.float32(1.5703125)
+    rest = rest - turns * np.float32(4.837512969970703125e-4)
+    rest = rest - turns * np.float32(7.54978995489188216e-8)
+    square = rest * rest
+    sine = rest + rest * square * (
+        np.float32(-1.6666654611e-1)
+        + square * (np.float32(8.3321608736e-3) + square * np.float32(-1.9515295891e-4))
+    )
+    cosine = (
+        1.0
+        - 0.5 * square
+        + square
+        * square
+        * (
+            np.float32(4.166664568298827e-2)
+            + square * (np.float32(-1.388731625493765e-3) + square * np.float32(2.443315711809948e-5))
+        )
+    )
+    quarter = turns.astype(jnp.int32)
+    swap = (quarter & 1) == 1
+    out_cos = jnp.where(swap, sine, cosine)
+    out_sin = jnp.where(swap, cosine, sine)
+    out_cos = jnp.where(((quarter + 1) & 2) == 2, -out_cos, out_cos)
+    out_sin = jnp.where((quarter & 2) == 2, -out_sin, out_sin)
+    return out_cos, out_sin
+
+
+def split(value):
+    high = value.astype(jnp.bfloat16)
+    return high, (value - high.astype(jnp.float32)).astype(jnp.bfloat16)
+
+
+def fused_kernel(
+    counts,
+    phase,
+    direction,
+    tilts,
+    mask_hbm,
+    wind_hbm,
+    noise_hbm,
+    table_hbm,
+    out,
+    curvature,
+    send_lines,
+    lines,
+    send_tilt,
+    tilt_tiles,
+    extended,
+    mask,
+    wind,
+    noise,
+    table,
+    packed_mask,
+    packed_noise,
+    turn,
+    field,
+    operand,
+    image,
+    push,
+    dir_wide,
+    bent,
+    prior,
+    near,
+    send_grad,
+    grads,
+    parts,
+    local_sem,
+    line_send,
+    line_recv,
+    halo_send,
+    halo_recv,
+    grad_send,
+    grad_recv,
+    part_send,
+    part_recv,
+):
+    tm_count, mod_count = counts
+    frames, width, rows = phase.shape
+    chunks = mod_count // frames
+    chunk = rows // chunks
+    pieces = chunks
+    sub = width // pieces
+    pupil = width * mod_count
+    length = 2 * pupil
+    packed_rows = pupil // pieces
+    half = pupil // 2
+    groups = mod_count // pieces
+    lanes = groups * rows
+    tm = lax.axis_index("tm")
+    mod = lax.axis_index("mod")
+    own_frame = mod // chunks
+    own_chunk = mod % chunks
+
+    copies = [
+        pltpu.make_async_copy(noise_hbm.at[own_frame], noise, local_sem.at[0]),
+        pltpu.make_async_copy(mask_hbm, mask, local_sem.at[1]),
+        pltpu.make_async_copy(wind_hbm, wind, local_sem.at[2]),
+        pltpu.make_async_copy(table_hbm, table, local_sem.at[3]),
+    ]
+
+    barrier = pltpu.get_barrier_semaphore()
+    peers = [
+        (a, b) for a in range(tm_count) for b in range(mod_count) if (a, b) != (0, 0)
+    ]
+
+    def peer(a, b):
+        return {"tm": (tm + a) % tm_count, "mod": (mod + b) % mod_count}
+
+    for a, b in peers:
+        pl.semaphore_signal(
+            barrier, inc=1, device_id=peer(a, b), device_id_type=pl.DeviceIdType.MESH
+        )
+    for copy in copies:
+        copy.start()
+
+    lane_group = lax.broadcasted_iota(jnp.int32, (TILE, rows), 1) // chunk
+
+    def at_lanes(values):
+        out_value = values[0]
+        for j in range(1, len(values)):
+            out_value = jnp.where(lane_group[: out_value.shape[0]] == j, values[j], out_value)
+        return out_value
+
+    def turned(value, amount):
+        if isinstance(amount, int):
+            amount = amount % rows
+            if amount == 0:
+                return value
+        return pltpu.roll(value, amount, 1)
+
+    def widened(value):
+        shifts = [turned(value, s * chunk) for s in range(pieces)]
+        return [
+            at_lanes([shifts[(m - j) % pieces] for m in range(pieces)]) for j in range(pieces)
+        ]
+
+    def over_groups(value):
+        step = chunk
+        while step < rows:
+            value = value + pltpu.roll(value, step, 1)
+            step *= 2
+        return value
+
+    def tiles(n, body, unroll=2):
+        def step(i, carry):
+            body(pl.multiple_of(i * TILE, TILE))
+            return carry
+
+        lax.fori_loop(0, n // TILE, step, 0, unroll=unroll)
+
+    send_tilt[...] = jnp.full(send_tilt.shape, tilts[0].astype(jnp.float32))
+    for which, source in enumerate((phase, direction)):
+        for f in range(frames):
+            for base in range(0, sub, TILE):
+                loaded = [
+                    source[f, pl.ds(base * pieces + j, TILE, stride=pieces), :]
+                    for j in range(pieces)
+                ]
+                for k in range(chunks):
+                    send_lines[which, f * chunks + k, base : base + TILE] = at_lanes(
+                        [turned(loaded[j], (j - k) * chunk) for j in range(pieces)]
+                    )
+
+    pl.semaphore_wait(barrier, len(peers))
+
+    my_lines = pl.ds(pl.multiple_of(mod * sub, sub), sub)
+    tilt_copies, line_copies = [], [[], []]
+    for o in range(1, mod_count):
+        tilt_copies.append(
+            pltpu.make_async_remote_copy(
+                send_tilt,
+                tilt_tiles.at[mod],
+                line_send.at[2, o - 1],
+                line_recv.at[2, o - 1],
+                device_id=peer(0, o),
+                device_id_type=pl.DeviceIdType.MESH,
+            )
+        )
+        for which in range(2):
+            line_copies[which].append(
+                pltpu.make_async_remote_copy(
+                    send_lines.at[which, (mod + o) % mod_count],
+                    lines.at[which, my_lines],
+                    line_send.at[which, o - 1],
+                    line_recv.at[which, o - 1],
+                    device_id=peer(0, o),
+                    device_id_type=pl.DeviceIdType.MESH,
+                )
+            )
+    for copy in tilt_copies + line_copies[0]:
+        copy.start()
+
+    halos = []
+    for da in (-1, 0, 1):
+        for db in (-1, 0, 1):
+            if (da, db) == (0, 0):
+                continue
+            src_f, dst_f, n_f = {1: (frames - 1, 0, 1), 0: (0, 1, frames), -1: (0, frames + 1, 1)}[da]
+            src_x, dst_x, n_x = {
+                1: (width - HALO, 0, HALO),
+                0: (0, HALO, width),
+                -1: (0, HALO + width, HALO),
+            }[db]
+            slot = len(halos)
+            copy = pltpu.make_async_remote_copy(
+                direction.at[pl.ds(src_f, n_f), pl.ds(src_x, n_x)],
+                extended.at[pl.ds(dst_f, n_f), pl.ds(dst_x, n_x)],
+                halo_send.at[slot],
+                halo_recv.at[slot],
+                device_id=peer(da, db),
+                device_id_type=pl.DeviceIdType.MESH,
+            )
+            sends = (tm + da >= 0) & (tm + da < tm_count) & (mod + db >= 0) & (mod + db < mod_count)
+            takes = (tm - da >= 0) & (tm - da < tm_count) & (mod - db >= 0) & (mod - db < mod_count)
+            halos.append((copy, sends, takes, (dst_f, n_f, dst_x, n_x)))
+            pl.when(sends)(copy.start)
+    for copy in line_copies[1]:
+        copy.start()
+
+    for which in range(2):
+        lines[which, my_lines] = send_lines[which, mod]
+    tilt_tiles[mod] = send_tilt[...]
+    extended[1 : 1 + frames, HALO : HALO + width] = direction[...]
+    for _, _, takes, (dst_f, n_f, dst_x, n_x) in halos:
+
+        @pl.when(jnp.logical_not(takes))
+        def _():
+            extended[dst_f : dst_f + n_f, dst_x : dst_x + n_x] = jnp.zeros(
+                (n_f, n_x, rows), jnp.float32
+            )
+
+    copies[1].wait()
+    copies[0].wait()
+
+    def pack_own(source, base, row):
+        return at_lanes(
+            [
+                pltpu.roll(
+                    source[pl.ds(base + row * pieces + j, TILE, stride=pieces), :],
+                    ((j + chunks - own_chunk) % chunks) * chunk,
+                    1,
+                )
+                for j in range(pieces)
+            ]
+        )
+
+    def pack_rows(row):
+        packed_mask[pl.ds(row, TILE)] = pack_own(mask, 0, row).astype(jnp.float32)
+        for side in range(2):
+            packed_noise[side, pl.ds(row, TILE)] = pack_own(noise, side * pupil, row)
+
+    tiles(packed_rows, pack_rows)
+
+    for copy in tilt_copies:
+        copy.wait_recv()
+
+    def turn_rows(row):
+        for l in range(groups):
+            tilt = at_lanes([tilt_tiles[l * pieces + m] for m in range(pieces)]).astype(jnp.int32)
+            tilt = jnp.concatenate([tilt] * (TILE // tilt.shape[0]), axis=0)
+            index = row + lax.broadcasted_iota(jnp.int32, (TILE, rows), 0)
+            for j in range(pieces):
+                position = half + pieces * index + j
+                product = tilt * position
+                if length & (length - 1) == 0:
+                    product = product & (length - 1)
+                else:
+                    product = product % length
+                cosine, sine = cos_sin(
+                    np.float32(2.0 * np.pi / length) * product.astype(jnp.float32)
+                )
+                turn[0, j, pl.ds(row, TILE), l * rows : (l + 1) * rows] = cosine
+                turn[1, j, pl.ds(row, TILE), l * rows : (l + 1) * rows] = sine
+
+    tiles(packed_rows, turn_rows)
+
+    def place(j, row):
+        return j % 2, pl.ds(pl.multiple_of((j // 2) * packed_rows + row, TILE), TILE)
+
+    def put_operand(j, row, l, real, imag):
+        for part, value in enumerate((real, imag)):
+            parity, _ = place(j, row)
+            high, low = split(value)
+            columns = slice(part * lanes + l * rows, part * lanes + (l + 1) * rows)
+            start = (j // 2) * packed_rows + row
+            for copy_index, item in enumerate((high, low, high)):
+                operand[parity, pl.ds(pl.multiple_of(copy_index * half + start, TILE), TILE), columns] = item
+
+    def couple(target):
+        for parity in range(2):
+            target[1 - parity] = jnp.dot(
+                table[parity], operand[parity], preferred_element_type=jnp.float32
+            )
+
+    def columns_of(part, l):
+        return slice(part * lanes + l * rows, part * lanes + (l + 1) * rows)
+
+    for copy in line_copies[0]:
+        copy.wait_recv()
+
+    def field_rows(row):
+        cosine, sine = cos_sin(lines[0, pl.ds(row, TILE)])
+        lit = packed_mask[pl.ds(row, TILE)]
+        wide_cos, wide_sin = widened(cosine * lit), widened(sine * lit)
+        for j in range(pieces):
+            parity, where = place(j, row)
+            for l in range(groups):
+                turn_cos = turn[0, j, pl.ds(row, TILE), l * rows : (l + 1) * rows]
+                turn_sin = turn[1, j, pl.ds(row, TILE), l * rows : (l + 1) * rows]
+                real = wide_cos[j] * turn_cos - wide_sin[j] * turn_sin
+                imag = wide_cos[j] * turn_sin + wide_sin[j] * turn_cos
+                field[parity, where, columns_of(0, l)] = real
+                field[parity, where, columns_of(1, l)] = imag
+                put_operand(j, row, l, real, imag)
+
+    tiles(packed_rows, field_rows)
+    copies[3].wait()
+    couple(image)
+
+    copies[2].wait()
+    for copy, _, takes, _ in halos:
+        pl.when(takes)(copy.wait_recv)
+    before = pl.ds(
+        pl.multiple_of(((mod + mod_count - 1) % mod_count) * width + (width - HALO), HALO), HALO
+    )
+    codes = jnp.concatenate(
+        [wind[before], wind[pl.ds(pl.multiple_of(mod * width, HALO), width)]], axis=0
+    )
+    tall = HALO + width
+    frac_x = ((codes & 3).astype(jnp.float32) + 0.5) * 0.25
+    frac_r = ((codes >> 2).astype(jnp.float32) + 0.5) * 0.25
+    stay_stay = (1.0 - frac_x) * (1.0 - frac_r)
+    ahead_stay = frac_x * (1.0 - frac_r)
+    stay_ahead = (1.0 - frac_x) * frac_r
+    ahead_ahead = frac_x * frac_r
+    lane = lax.broadcasted_iota(jnp.int32, (tall, rows), 1)
+    pixel = mod * width - HALO + lax.broadcasted_iota(jnp.int32, (tall, rows), 0)
+    total_frames = frames * tm_count
+    for i in range(frames + 1):
+        base = extended[i, 0:tall]
+        ahead = extended[i, 1 : tall + 1]
+        crossing = stay_ahead * jnp.where(lane == rows - 1, 0.0, pltpu.roll(base, rows - 1, 1))
+        crossing += ahead_ahead * jnp.where(lane == rows - 1, 0.0, pltpu.roll(ahead, rows - 1, 1))
+        moved = stay_stay * base + ahead_stay * ahead + crossing
+        flow_id = tm * frames - 1 + i
+        valid = (pixel >= 0) & (flow_id >= 0) & (flow_id <= total_frames - 2)
+        flow = jnp.where(valid, extended[i + 1, 0:tall] - moved, 0.0)
+        if i >= 1:
+            near[0] = ahead_stay * flow
+            near[1] = ahead_ahead * flow
+            behind = (stay_ahead * flow)[HALO:] + near[1, HALO - 1 : HALO - 1 + width]
+            spread = (
+                (stay_stay * flow)[HALO:]
+                + near[0, HALO - 1 : HALO - 1 + width]
+                + jnp.where(lane[HALO:] == 0, 0.0, pltpu.roll(behind, 1, 1))
+            )
+            prior[i - 1] = prior[i - 1] - spread
+        if i < frames:
+            prior[i] = flow[HALO:]
+
+    for copy in line_copies[1]:
+        copy.wait_recv()
+
+    def dir_rows(row):
+        wide = widened(lines[1, pl.ds(row, TILE)])
+        for j in range(pieces):
+            parity, where = place(j, row)
+            dir_wide[parity, where] = wide[j]
+            for l in range(groups):
+                real = field[parity, where, columns_of(0, l)] * wide[j]
+                imag = field[parity, where, columns_of(1, l)] * wide[j]
+                put_operand(j, row, l, real, imag)
+
+    tiles(packed_rows, dir_rows)
+    couple(push)
+
+    def signal_rows(row):
+        wide_noise = [widened(packed_noise[side, pl.ds(row, TILE)]) for side in range(2)]
+        for j in range(pieces):
+            parity, where = place(j, row)
+            step = dir_wide[parity, where]
+            even = odd = None
+            for l in range(groups):
+                er = field[parity, where, columns_of(0, l)]
+                ei = field[parity, where, columns_of(1, l)]
+                ur = image[parity, where, columns_of(0, l)]
+                ui = image[parity, where, columns_of(1, l)]
+                vr = push[parity, where, columns_of(0, l)]
+                vi = push[parity, where, columns_of(1, l)]
+                even_l = ui * vr - ur * vi
+                odd_l = (ur * er + ui * ei) * step - (er * vr + ei * vi)
+                even = even_l if even is None else even + even_l
+                odd = odd_l if odd is None else odd + odd_l
+            even = 2.0 * over_groups(even)
+            odd = over_groups(odd)
+            front = wide_noise[0][j] * (even + odd)
+            back = wide_noise[1][j] * (even - odd)
+            both = front + back
+            differ = 0.5 * (front - back)
+            bent[parity, where] = differ
+            for l in range(groups):
+                er = field[parity, where, columns_of(0, l)]
+                ei = field[parity, where, columns_of(1, l)]
+                ur = image[parity, where, columns_of(0, l)]
+                ui = image[parity, where, columns_of(1, l)]
+                put_operand(j, row, l, differ * er - both * ui, differ * ei + both * ur)
+
+    tiles(packed_rows, signal_rows)
+    couple(push)
+
+    parts_own = tm * mod_count + mod
+
+    def grad_rows(i, total):
+        row = pl.multiple_of(i * TILE, TILE)
+        grad = []
+        for j in range(pieces):
+            parity, where = place(j, row)
+            differ = bent[parity, where]
+            acc = None
+            for l in range(groups):
+                er = field[parity, where, columns_of(0, l)]
+                ei = field[parity, where, columns_of(1, l)]
+                kr = differ * image[parity, where, columns_of(0, l)] + push[parity, where, columns_of(0, l)]
+                ki = differ * image[parity, where, columns_of(1, l)] + push[parity, where, columns_of(1, l)]
+                term = er * kr + ei * ki
+                acc = term if acc is None else acc + term
+            grad.append(2.0 * over_groups(acc))
+        packed = at_lanes(grad)
+        send_grad[pl.ds(row, TILE)] = packed
+        return total + packed * lines[1, pl.ds(row, TILE)]
+
+    total = lax.fori_loop(
+        0, packed_rows // TILE, grad_rows, jnp.zeros((TILE, rows), jnp.float32), unroll=2
+    )
+    total = total[:HALO] + total[HALO:]
+    for f in range(frames):
+        for base in range(0, width, HALO):
+            total = total + prior[f, base : base + HALO] * direction[f, base : base + HALO]
+    parts[parts_own] = total
+
+    grad_copies = []
+    for o in range(1, mod_count):
+        owner = (mod + o) % mod_count
+        grad_copies.append(
+            pltpu.make_async_remote_copy(
+                send_grad.at[pl.ds(pl.multiple_of(owner * sub, sub), sub)],
+                grads.at[mod],
+                grad_send.at[o - 1],
+                grad_recv.at[o - 1],
+                device_id=peer(0, o),
+                device_id_type=pl.DeviceIdType.MESH,
+            )
+        )
+        grad_copies[-1].start()
+    part_copies = []
+    for slot, (a, b) in enumerate(peers):
+        part_copies.append(
+            pltpu.make_async_remote_copy(
+                parts.at[parts_own],
+                parts.at[parts_own],
+                part_send.at[slot],
+                part_recv.at[slot],
+                device_id=peer(a, b),
+                device_id_type=pl.DeviceIdType.MESH,
+            )
+        )
+        part_copies[-1].start()
+    grads[mod] = send_grad[my_lines]
+
+    for copy in tilt_copies + line_copies[0] + line_copies[1]:
+        copy.wait_send()
+    for copy, sends, _, _ in halos:
+        pl.when(sends)(copy.wait_send)
+    for copy in grad_copies:
+        copy.wait()
+
+    for f in range(frames):
+        for base in range(0, sub, TILE):
+            arrived = [grads[f * chunks + k, base : base + TILE] for k in range(chunks)]
+            for j in range(pieces):
+                where = pl.ds(base * pieces + j, TILE, stride=pieces)
+                grad = at_lanes([turned(arrived[k], (k - j) * chunk) for k in range(chunks)])
+                out[f, where, :] = grad + prior[f, where, :]
+
+    for copy in part_copies:
+        copy.wait()
+    whole = parts[0]
+    for n in range(1, tm_count * mod_count):
+        whole = whole + parts[n]
+    entries = float(total_frames * pupil * rows)
+    curvature[0] = jnp.sum(whole) / entries
+
+
+def fused_device(phase, direction, pupil_mask, mod_tilts, wind_codes, noise_weight):
+    frames, width, rows = phase.shape
+    tm_count, mod_count = lax.axis_size("tm"), lax.axis_size("mod")
+    pieces = mod_count // frames
+    sub = width // pieces
+    pupil = width * mod_count
+    half = pupil // 2
+    lanes = mod_count // pieces * rows
+    packed_rows = pupil // pieces
+    everyone = tm_count * mod_count
+    vmem, smem, hbm = (
+        pl.BlockSpec(memory_space=pltpu.VMEM),
+        pl.BlockSpec(memory_space=pltpu.SMEM),
+        pl.BlockSpec(memory_space=pl.ANY),
+    )
+    f32, bf16 = jnp.float32, jnp.bfloat16
+    dma = pltpu.SemaphoreType.DMA
+    return pl.pallas_call(
+        functools.partial(fused_kernel, (tm_count, mod_count)),
+        out_shape=(
+            jax.ShapeDtypeStruct(phase.shape, f32),
+            jax.ShapeDtypeStruct((1,), f32),
+        ),
+        in_specs=[vmem, vmem, smem, hbm, hbm, hbm, hbm],
+        out_specs=(vmem, smem),
+        scratch_shapes=[
+            pltpu.VMEM((2, mod_count, sub, rows), f32),
+            pltpu.VMEM((2, packed_rows, rows), f32),
+            pltpu.VMEM((8, rows), f32),
+            pltpu.VMEM((mod_count, 8, rows), f32),
+            pltpu.VMEM((frames + 2, width + 2 * HALO, rows), f32),
+            pltpu.VMEM(pupil_mask.shape, jnp.int32),
+            pltpu.VMEM(wind_codes.shape, jnp.int32),
+            pltpu.VMEM(noise_weight.shape[1:], f32),
+            pltpu.VMEM((2, half, 3 * half), bf16),
+            pltpu.VMEM((packed_rows, rows), f32),
+            pltpu.VMEM((2, packed_rows, rows), f32),
+            pltpu.VMEM((2, pieces, packed_rows, lanes), f32),
+            pltpu.VMEM((2, half, 2 * lanes), f32),
+            pltpu.VMEM((2, 3 * half, 2 * lanes), bf16),
+            pltpu.VMEM((2, half, 2 * lanes), f32),
+            pltpu.VMEM((2, half, 2 * lanes), f32),
+            pltpu.VMEM((2, half, rows), f32),
+            pltpu.VMEM((2, half, rows), f32),
+            pltpu.VMEM((frames, width, rows), f32),
+            pltpu.VMEM((2, width + HALO, rows), f32),
+            pltpu.VMEM((packed_rows, rows), f32),
+            pltpu.VMEM((mod_count, sub, rows), f32),
+            pltpu.VMEM((everyone, 8, rows), f32),
+            dma((4,)),
+            dma((3, mod_count - 1)),
+            dma((3, mod_count - 1)),
+            dma((8,)),
+            dma((8,)),
+            dma((mod_count - 1,)),
+            dma((mod_count - 1,)),
+            dma((everyone - 1,)),
+            dma((everyone - 1,)),
+        ],
+        compiler_params=pltpu.CompilerParams(collective_id=0, has_side_effects=True),
+    )(
+        phase,
+        direction,
+        mod_tilts,
+        pupil_mask,
+        wind_codes,
+        noise_weight,
+        jnp.asarray(coupling_tables(pupil, pieces)),
+    )
+
+
+def device_program(phase, direction, pupil_mask, mod_tilts, wind_codes, noise_weight):
+    frames, width, rows = phase.shape
+    mod_count = lax.axis_size("mod")
+    fits = mod_count % frames == 0 and mod_tilts.shape[0] == 1 and frames > 1
+    if fits:
+        pieces = mod_count // frames
+        fits = (
+            pieces % 2 == 0
+            and rows == 128
+            and rows % pieces == 0
+            and width % (pieces * TILE) == 0
+            and pieces & (pieces - 1) == 0
+        )
+    run = fused_device if fits else per_device
+    return run(phase, direction, pupil_mask, mod_tilts, wind_codes, noise_weight)
+
+
 def solution(mesh):
     return jax.shard_map(
-        per_device,
+        device_program,
         mesh=mesh,
         in_specs=(
             P(("grp", "tm"), "mod", None),

time: 238 us -> 26.9 us (0.11); the launches traced: 235 us -> 26.7 us
  matrix products: 80.7 us -> 0 us
  waiting for transfers between devices: 55.8 us -> 0 us
  blocking collectives: 42.1 us -> 0 us
  Pallas kernels: 0 us -> 22 us
  other arithmetic: 16.2 us -> 0 us
  local copies, waits for them, and re-layouts: 16.5 us -> 1.57 us
  between operations: 17.1 us -> 3.1 us
  starting transfers between devices: 6.66 us -> 0 us
    dot_general x48 -> x0, matrix products: 80.7 us -> none  [the longest x12 21.3 us: complex_mix(): imag_real = jnp.einsum(form, table_imag, field_real, precision=HIGHEST)]
    psum x1 -> x0, blocking collectives: 32.7 us -> none  [per_device(): curvature_total = lax.psum(jnp.sum(direction * hess_vec), ('tm', 'mod'))]
    psum x1 -> x0, waiting for transfers between devices: 30.4 us -> none  [per_device(): signal_full = lax.psum(signal_local, 'mod')]
    pallas_call x0 -> x1, Pallas kernels: none -> 22 us  [fused_device(): pl.pallas_call(functools.partial(fused_kernel, (tm_count, mod_count)), ou...]
    reduce_scatter x1 -> x0, waiting for transfers between devices: 18.2 us -> none  [per_device(): lax.psum_scatter(grad_lines, 'mod', scatter_dimension=1, tiled=True)]
    all_gather x1 -> x0, blocking collectives: 9.45 us -> none  [per_device(): lax.all_gather(phase, 'mod', axis=1, tiled=True)]
    mul x6 -> x0, other arithmetic: 8.21 us -> none  [the longest x1 4.07 us: forward_pass(): -field_imag * full_direction]
    slice x9 -> x0, local copies, waits for them, and re-layouts: 7.5 us -> none  [the longest x1 1.96 us: row_ahead(): return jnp.pad(field[:, :, 1:], ((0, 0), (0, 0), (0, 1)))]
  transfers between devices with their start and end apart: 5 -> 0, of which waited for: 4 -> 0; matrix products, arithmetic and copies ran while one was open for 5% -> 0% of each run, Pallas kernels for 0% -> 0%
where the time goes in v1:
time: 26.9 us; the launch traced here: 26.7 us
  Pallas kernels  22 us (82%)
  between operations  3.1 us (12%)
  local copies, waits for them, and re-layouts  1.57 us (6%)
    pallas_call x1, Pallas kernels, fused_device(): pl.pallas_call(functools.partial(fused_kernel, (tm_count, mod_count)), ou...  22 us
    unnamed x1, local copies, waits for them, and re-layouts  1.57 us

profile of v1, /device:TPU:0, one launch (start us, length us, event | category | flops | bytes accessed | tf_op | source)
XLA Modules:
  0.0 26.7 jit_solution(4067513458507079620)
XLA Ops:
  1.3 22.0 %shard_map.86 = (f32[2,128,128]{2,1,0:T(8,128)}, f32[1]{0:T(128)}) custom-call(f32[2,128,128]{2,1,0:T(8,128)} %phase.1, f32[2,128,128]{2,1,0:T(8,128)} %direction.1, s32[1]{0:T(128)S(6)} %copy.11.tilts, s32[512,128]{1,0:T(8,128)} %mask_hbm.1, s32[512,128]{1,0:T(8,128)} %wind_hbm.1, f32[2,1024,128]{2,1,0:T(8,128)} %noise_hbm.1, ...), custom_call_target="tpu_custom_call" | custom-call | tf_op jit(solution)/shard_map/pallas_call | solution.py:762
  23.3 1.6 %copy.12 = f32[2,128,128]{2,1,0:T(8,128)} copy(f32[2,128,128]{2,1,0:T(8,128)} %get-tuple-element.4) | data formatting | bytes 262144

commit v2 on v1

--- a/solution.py
+++ b/solution.py
@@ -285,13 +285,14 @@
     counts,
     phase,
     direction,
-    tilts,
+    tilts_hbm,
     mask_hbm,
     wind_hbm,
     noise_hbm,
     table_hbm,
-    out,
-    curvature,
+    grads,
+    prior,
+    parts,
     send_lines,
     lines,
     send_tilt,
@@ -310,11 +311,9 @@
     push,
     dir_wide,
     bent,
-    prior,
     near,
     send_grad,
-    grads,
-    parts,
+    tilts,
     local_sem,
     line_send,
     line_recv,
@@ -324,6 +323,7 @@
     grad_recv,
     part_send,
     part_recv,
+    entered,
 ):
     tm_count, mod_count = counts
     frames, width, rows = phase.shape
@@ -347,6 +347,7 @@
         pltpu.make_async_copy(mask_hbm, mask, local_sem.at[1]),
         pltpu.make_async_copy(wind_hbm, wind, local_sem.at[2]),
         pltpu.make_async_copy(table_hbm, table, local_sem.at[3]),
+        pltpu.make_async_copy(tilts_hbm, tilts, local_sem.at[4]),
     ]
 
     barrier = pltpu.get_barrier_semaphore()
@@ -357,10 +358,35 @@
     def peer(a, b):
         return {"tm": (tm + a) % tm_count, "mod": (mod + b) % mod_count}
 
-    for a, b in peers:
+    for b in range(1, mod_count):
         pl.semaphore_signal(
-            barrier, inc=1, device_id=peer(a, b), device_id_type=pl.DeviceIdType.MESH
+            barrier, inc=1, device_id=peer(0, b), device_id_type=pl.DeviceIdType.MESH
         )
+    beside = [(-1, tm > 0), (1, tm < tm_count - 1)]
+
+    def tell_beside(semaphores):
+        for side, (step, exists) in enumerate(beside):
+
+            @pl.when(exists)
+            def _():
+                pl.semaphore_signal(
+                    semaphores[1 - side],
+                    inc=1,
+                    device_id=peer(step, 0),
+                    device_id_type=pl.DeviceIdType.MESH,
+                )
+
+    def hear_beside(semaphores):
+        for side, (step, exists) in enumerate(beside):
+
+            @pl.when(exists)
+            def _():
+                pl.semaphore_wait(semaphores[side], 1)
+
+    def entered_at(n):
+        return [entered.at[n, 0], entered.at[n, 1]]
+
+    tell_beside([barrier, barrier])
     for copy in copies:
         copy.start()
 
@@ -399,7 +425,6 @@
 
         lax.fori_loop(0, n // TILE, step, 0, unroll=unroll)
 
-    send_tilt[...] = jnp.full(send_tilt.shape, tilts[0].astype(jnp.float32))
     for which, source in enumerate((phase, direction)):
         for f in range(frames):
             for base in range(0, sub, TILE):
@@ -412,7 +437,10 @@
                         [turned(loaded[j], (j - k) * chunk) for j in range(pieces)]
                     )
 
-    pl.semaphore_wait(barrier, len(peers))
+    copies[4].wait()
+    send_tilt[...] = jnp.full(send_tilt.shape, tilts[0].astype(jnp.float32))
+    earlier, later = (tm + tm_count - 1) // tm_count, (2 * tm_count - 2 - tm) // tm_count
+    pl.semaphore_wait(barrier, mod_count - 1 + earlier + later)
 
     my_lines = pl.ds(pl.multiple_of(mod * sub, sub), sub)
     tilt_copies, line_copies = [], [[], []]
@@ -440,8 +468,9 @@
             )
     for copy in tilt_copies + line_copies[0]:
         copy.start()
-
-    halos = []
+    tell_beside(entered_at(0))
+
+    halos, corners = [], []
     for da in (-1, 0, 1):
         for db in (-1, 0, 1):
             if (da, db) == (0, 0):
@@ -464,7 +493,10 @@
             sends = (tm + da >= 0) & (tm + da < tm_count) & (mod + db >= 0) & (mod + db < mod_count)
             takes = (tm - da >= 0) & (tm - da < tm_count) & (mod - db >= 0) & (mod - db < mod_count)
             halos.append((copy, sends, takes, (dst_f, n_f, dst_x, n_x)))
-            pl.when(sends)(copy.start)
+            if da == 0 or db == 0:
+                pl.when(sends)(copy.start)
+            else:
+                corners.append((copy, sends))
     for copy in line_copies[1]:
         copy.start()
 
@@ -502,6 +534,11 @@
 
     tiles(packed_rows, pack_rows)
 
+    hear_beside(entered_at(0))
+    for copy, sends in corners:
+        pl.when(sends)(copy.start)
+    if tm_count > 2:
+        tell_beside(entered_at(1))
     for copy in tilt_copies:
         copy.wait_recv()
 
@@ -546,6 +583,10 @@
     def columns_of(part, l):
         return slice(part * lanes + l * rows, part * lanes + (l + 1) * rows)
 
+    for n in range(1, tm_count - 1):
+        hear_beside(entered_at(n))
+        if n < tm_count - 2:
+            tell_beside(entered_at(n + 1))
     for copy in line_copies[0]:
         copy.wait_recv()
 
@@ -587,6 +628,7 @@
     lane = lax.broadcasted_iota(jnp.int32, (tall, rows), 1)
     pixel = mod * width - HALO + lax.broadcasted_iota(jnp.int32, (tall, rows), 0)
     total_frames = frames * tm_count
+    flow_power = jnp.zeros((HALO, rows), jnp.float32)
     for i in range(frames + 1):
         base = extended[i, 0:tall]
         ahead = extended[i, 1 : tall + 1]
@@ -597,6 +639,8 @@
         valid = (pixel >= 0) & (flow_id >= 0) & (flow_id <= total_frames - 2)
         flow = jnp.where(valid, extended[i + 1, 0:tall] - moved, 0.0)
         if i >= 1:
+            for start in range(HALO, tall, HALO):
+                flow_power += flow[start : start + HALO] * flow[start : start + HALO]
             near[0] = ahead_stay * flow
             near[1] = ahead_ahead * flow
             behind = (stay_ahead * flow)[HALO:] + near[1, HALO - 1 : HALO - 1 + width]
@@ -625,7 +669,8 @@
     tiles(packed_rows, dir_rows)
     couple(push)
 
-    def signal_rows(row):
+    def signal_rows(i, power):
+        row = pl.multiple_of(i * TILE, TILE)
         wide_noise = [widened(packed_noise[side, pl.ds(row, TILE)]) for side in range(2)]
         for j in range(pieces):
             parity, where = place(j, row)
@@ -646,6 +691,7 @@
             odd = over_groups(odd)
             front = wide_noise[0][j] * (even + odd)
             back = wide_noise[1][j] * (even - odd)
+            power = power + front * (even + odd) + back * (even - odd)
             both = front + back
             differ = 0.5 * (front - back)
             bent[parity, where] = differ
@@ -656,13 +702,29 @@
                 ui = image[parity, where, columns_of(1, l)]
                 put_operand(j, row, l, differ * er - both * ui, differ * ei + both * ur)
 
-    tiles(packed_rows, signal_rows)
+        return power
+
+    power = lax.fori_loop(
+        0, packed_rows // TILE, signal_rows, jnp.zeros((TILE, rows), jnp.float32), unroll=2
+    )
+    parts_own = tm * mod_count + mod
+    parts[parts_own] = (power[:HALO] + power[HALO:]) * (1.0 / pieces) + flow_power
+    part_copies = []
+    for slot, (a, b) in enumerate(peers):
+        part_copies.append(
+            pltpu.make_async_remote_copy(
+                parts.at[parts_own],
+                parts.at[parts_own],
+                part_send.at[slot],
+                part_recv.at[slot],
+                device_id=peer(a, b),
+                device_id_type=pl.DeviceIdType.MESH,
+            )
+        )
+        part_copies[-1].start()
     couple(push)
 
-    parts_own = tm * mod_count + mod
-
-    def grad_rows(i, total):
-        row = pl.multiple_of(i * TILE, TILE)
+    def grad_rows(row):
         grad = []
         for j in range(pieces):
             parity, where = place(j, row)
@@ -676,18 +738,9 @@
                 term = er * kr + ei * ki
                 acc = term if acc is None else acc + term
             grad.append(2.0 * over_groups(acc))
-        packed = at_lanes(grad)
-        send_grad[pl.ds(row, TILE)] = packed
-        return total + packed * lines[1, pl.ds(row, TILE)]
-
-    total = lax.fori_loop(
-        0, packed_rows // TILE, grad_rows, jnp.zeros((TILE, rows), jnp.float32), unroll=2
-    )
-    total = total[:HALO] + total[HALO:]
-    for f in range(frames):
-        for base in range(0, width, HALO):
-            total = total + prior[f, base : base + HALO] * direction[f, base : base + HALO]
-    parts[parts_own] = total
+        send_grad[pl.ds(row, TILE)] = at_lanes(grad)
+
+    tiles(packed_rows, grad_rows)
 
     grad_copies = []
     for o in range(1, mod_count):
@@ -703,42 +756,36 @@
             )
         )
         grad_copies[-1].start()
-    part_copies = []
-    for slot, (a, b) in enumerate(peers):
-        part_copies.append(
-            pltpu.make_async_remote_copy(
-                parts.at[parts_own],
-                parts.at[parts_own],
-                part_send.at[slot],
-                part_recv.at[slot],
-                device_id=peer(a, b),
-                device_id_type=pl.DeviceIdType.MESH,
-            )
-        )
-        part_copies[-1].start()
     grads[mod] = send_grad[my_lines]
 
     for copy in tilt_copies + line_copies[0] + line_copies[1]:
         copy.wait_send()
     for copy, sends, _, _ in halos:
         pl.when(sends)(copy.wait_send)
-    for copy in grad_copies:
+    for copy in grad_copies + part_copies:
         copy.wait()
 
+
+def gather_kernel(entries, grads, prior, parts, out, curvature):
+    frames, width, rows = prior.shape
+    mod_count, sub, _ = grads.shape
+    pieces = mod_count // frames
+    chunk = rows // pieces
+    lane_group = lax.broadcasted_iota(jnp.int32, (TILE, rows), 1) // chunk
     for f in range(frames):
         for base in range(0, sub, TILE):
-            arrived = [grads[f * chunks + k, base : base + TILE] for k in range(chunks)]
+            arrived = [grads[f * pieces + k, base : base + TILE] for k in range(pieces)]
             for j in range(pieces):
                 where = pl.ds(base * pieces + j, TILE, stride=pieces)
-                grad = at_lanes([turned(arrived[k], (k - j) * chunk) for k in range(chunks)])
+                grad = None
+                for k in range(pieces):
+                    shift = (k - j) * chunk % rows
+                    piece = pltpu.roll(arrived[k], shift, 1) if shift else arrived[k]
+                    grad = piece if grad is None else jnp.where(lane_group == k, piece, grad)
                 out[f, where, :] = grad + prior[f, where, :]
-
-    for copy in part_copies:
-        copy.wait()
     whole = parts[0]
-    for n in range(1, tm_count * mod_count):
+    for n in range(1, parts.shape[0]):
         whole = whole + parts[n]
-    entries = float(total_frames * pupil * rows)
     curvature[0] = jnp.sum(whole) / entries
 
 
@@ -757,16 +804,18 @@
         pl.BlockSpec(memory_space=pltpu.SMEM),
         pl.BlockSpec(memory_space=pl.ANY),
     )
+    fixed = pl.BlockSpec(memory_space=pltpu.HBM)
     f32, bf16 = jnp.float32, jnp.bfloat16
     dma = pltpu.SemaphoreType.DMA
-    return pl.pallas_call(
+    sums = pl.pallas_call(
         functools.partial(fused_kernel, (tm_count, mod_count)),
         out_shape=(
-            jax.ShapeDtypeStruct(phase.shape, f32),
-            jax.ShapeDtypeStruct((1,), f32),
+            pltpu.VMEM((mod_count, sub, rows), f32),
+            pltpu.VMEM(phase.shape, f32),
+            pltpu.VMEM((everyone, HALO, rows), f32),
         ),
-        in_specs=[vmem, vmem, smem, hbm, hbm, hbm, hbm],
-        out_specs=(vmem, smem),
+        in_specs=[vmem, vmem, fixed, hbm, hbm, hbm, hbm],
+        out_specs=(vmem, vmem, vmem),
         scratch_shapes=[
             pltpu.VMEM((2, mod_count, sub, rows), f32),
             pltpu.VMEM((2, packed_rows, rows), f32),
@@ -786,12 +835,10 @@
             pltpu.VMEM((2, half, 2 * lanes), f32),
             pltpu.VMEM((2, half, rows), f32),
             pltpu.VMEM((2, half, rows), f32),
-            pltpu.VMEM((frames, width, rows), f32),
             pltpu.VMEM((2, width + HALO, rows), f32),
             pltpu.VMEM((packed_rows, rows), f32),
-            pltpu.VMEM((mod_count, sub, rows), f32),
-            pltpu.VMEM((everyone, 8, rows), f32),
-            dma((4,)),
+            pltpu.SMEM((1,), jnp.int32),
+            dma((5,)),
             dma((3, mod_count - 1)),
             dma((3, mod_count - 1)),
             dma((8,)),
@@ -800,6 +847,7 @@
             dma((mod_count - 1,)),
             dma((everyone - 1,)),
             dma((everyone - 1,)),
+            pltpu.SemaphoreType.REGULAR((max(tm_count - 1, 1), 2)),
         ],
         compiler_params=pltpu.CompilerParams(collective_id=0, has_side_effects=True),
     )(
@@ -811,6 +859,12 @@
         noise_weight,
         jnp.asarray(coupling_tables(pupil, pieces)),
     )
+    return pl.pallas_call(
+        functools.partial(gather_kernel, float(frames * tm_count * pupil * rows)),
+        out_shape=(jax.ShapeDtypeStruct(phase.shape, f32), jax.ShapeDtypeStruct((1,), f32)),
+        in_specs=[vmem, vmem, vmem],
+        out_specs=(vmem, smem),
+    )(*[pltpu.with_memory_space_constraint(item, pltpu.VMEM) for item in sums])
 
 
 def device_program(phase, direction, pupil_mask, mod_tilts, wind_codes, noise_weight):
@@ -820,7 +874,8 @@
     if fits:
         pieces = mod_count // frames
         fits = (
-            pieces % 2 == 0
+            lax.axis_size("tm") > 1
+            and pieces % 2 == 0
             and rows == 128
             and rows % pieces == 0
             and width % (pieces * TILE) == 0

time: 26.9 us -> 21.5 us (0.80)
  Pallas kernels: 22 us -> 20 us
  between operations: 3.1 us -> 1.28 us
  local copies, waits for them, and re-layouts: 1.57 us -> 0 us
    pallas_call x1, Pallas kernels: 22 us -> 19.2 us  [fused_device(): pl.pallas_call(functools.partial(fused_kernel, (tm_count, mod_count)), ou...]
    unnamed x1 -> x0, local copies, waits for them, and re-layouts: 1.57 us -> none
    pallas_call x0 -> x1, Pallas kernels: none -> 0.79 us  [fused_device(): pl.pallas_call(functools.partial(gather_kernel, float(frames * tm_count *...]
where the time goes in v2:
time: 21.5 us; the launch traced here: 21.3 us
  Pallas kernels  20 us (93%)
  between operations  1.28 us (6%)
    pallas_call x1, Pallas kernels, fused_device(): pl.pallas_call(functools.partial(fused_kernel, (tm_count, mod_count)), ou...  19.2 us
    pallas_call x1, Pallas kernels, fused_device(): pl.pallas_call(functools.partial(gather_kernel, float(frames * tm_count *...  0.79 us

profile of v2, /device:TPU:0, one launch (start us, length us, event | category | flops | bytes accessed | tf_op | source)
XLA Modules:
  0.0 21.3 jit_solution(741233824875156181)
XLA Ops:
  1.3 19.2 %shard_map.86 = (f32[4,64,128]{2,1,0:T(8,128)S(1)}, f32[2,128,128]{2,1,0:T(8,128)S(1)}, f32[16,8,128]{2,1,0:T(8,128)S(1)}) custom-call(f32[2,128,128]{2,1,0:T(8,128)} %phase.1, f32[2,128,128]{2,1,0:T(8,128)} %direction.1, s32[1]{0:T(128)S(6)} %copy.9.tilts_hbm, s32[512,128]{1,0:T(8,128)} %mask_hbm.1, s32[512,128]{1,0:T(8,128)} %wind_hbm.1, ...), custom_call_target="tpu_custom_call" | custom-call | tf_op jit(solution)/shard_map/pallas_call | solution.py:810
  20.5 0.8 %shard_map.87 = (f32[2,128,128]{2,1,0:T(8,128)}, f32[1]{0:T(128)}) custom-call(f32[4,64,128]{2,1,0:T(8,128)S(1)} %get-tuple-element.5.grads, f32[2,128,128]{2,1,0:T(8,128)S(1)} %get-tuple-element.6.prior, f32[16,8,128]{2,1,0:T(8,128)S(1)} %get-tuple-element.7.parts), custom_call_target="tpu_custom_call" | custom-call | tf_op jit(solution)/shard_map/pallas_call | solution.py:862

commit v3 on v2

--- a/solution.py
+++ b/solution.py
@@ -283,9 +283,9 @@
 
 def fused_kernel(
     counts,
-    phase,
-    direction,
-    tilts_hbm,
+    phase_hbm,
+    direction_hbm,
+    tilts,
     mask_hbm,
     wind_hbm,
     noise_hbm,
@@ -313,7 +313,8 @@
     bent,
     near,
     send_grad,
-    tilts,
+    phase,
+    direction,
     local_sem,
     line_send,
     line_recv,
@@ -347,7 +348,8 @@
         pltpu.make_async_copy(mask_hbm, mask, local_sem.at[1]),
         pltpu.make_async_copy(wind_hbm, wind, local_sem.at[2]),
         pltpu.make_async_copy(table_hbm, table, local_sem.at[3]),
-        pltpu.make_async_copy(tilts_hbm, tilts, local_sem.at[4]),
+        pltpu.make_async_copy(phase_hbm, phase, local_sem.at[4]),
+        pltpu.make_async_copy(direction_hbm, direction, local_sem.at[5]),
     ]
 
     barrier = pltpu.get_barrier_semaphore()
@@ -387,7 +389,7 @@
         return [entered.at[n, 0], entered.at[n, 1]]
 
     tell_beside([barrier, barrier])
-    for copy in copies:
+    for copy in copies[4:] + copies[:4]:
         copy.start()
 
     lane_group = lax.broadcasted_iota(jnp.int32, (TILE, rows), 1) // chunk
@@ -426,6 +428,7 @@
         lax.fori_loop(0, n // TILE, step, 0, unroll=unroll)
 
     for which, source in enumerate((phase, direction)):
+        copies[4 + which].wait()
         for f in range(frames):
             for base in range(0, sub, TILE):
                 loaded = [
@@ -437,8 +440,7 @@
                         [turned(loaded[j], (j - k) * chunk) for j in range(pieces)]
                     )
 
-    copies[4].wait()
-    send_tilt[...] = jnp.full(send_tilt.shape, tilts[0].astype(jnp.float32))
+    send_tilt[...] = jnp.broadcast_to(tilts[...].astype(jnp.float32), send_tilt.shape)
     earlier, later = (tm + tm_count - 1) // tm_count, (2 * tm_count - 2 - tm) // tm_count
     pl.semaphore_wait(barrier, mod_count - 1 + earlier + later)
 
@@ -804,7 +806,6 @@
         pl.BlockSpec(memory_space=pltpu.SMEM),
         pl.BlockSpec(memory_space=pl.ANY),
     )
-    fixed = pl.BlockSpec(memory_space=pltpu.HBM)
     f32, bf16 = jnp.float32, jnp.bfloat16
     dma = pltpu.SemaphoreType.DMA
     sums = pl.pallas_call(
@@ -814,7 +815,7 @@
             pltpu.VMEM(phase.shape, f32),
             pltpu.VMEM((everyone, HALO, rows), f32),
         ),
-        in_specs=[vmem, vmem, fixed, hbm, hbm, hbm, hbm],
+        in_specs=[hbm, hbm, vmem, hbm, hbm, hbm, hbm],
         out_specs=(vmem, vmem, vmem),
         scratch_shapes=[
             pltpu.VMEM((2, mod_count, sub, rows), f32),
@@ -837,8 +838,9 @@
             pltpu.VMEM((2, half, rows), f32),
             pltpu.VMEM((2, width + HALO, rows), f32),
             pltpu.VMEM((packed_rows, rows), f32),
-            pltpu.SMEM((1,), jnp.int32),
-            dma((5,)),
+            pltpu.VMEM(phase.shape, f32),
+            pltpu.VMEM(direction.shape, f32),
+            dma((6,)),
             dma((3, mod_count - 1)),
             dma((3, mod_count - 1)),
             dma((8,)),
@@ -853,7 +855,7 @@
     )(
         phase,
         direction,
-        mod_tilts,
+        mod_tilts.reshape(1, 1),
         pupil_mask,
         wind_codes,
         noise_weight,

time: 21.5 us -> 20.6 us (0.958)
  Pallas kernels: 20 us -> 19.1 us
    pallas_call x1, Pallas kernels: 19.2 us -> 18.3 us  [fused_device(): pl.pallas_call(functools.partial(fused_kernel, (tm_count, mod_count)), ou...]
where the time goes in v3:
time: 20.6 us; the launch traced here: 20.4 us
  Pallas kernels  19.1 us (93%)
  between operations  1.28 us (6%)
    pallas_call x1, Pallas kernels, fused_device(): pl.pallas_call(functools.partial(fused_kernel, (tm_count, mod_count)), ou...  18.3 us
    pallas_call x1, Pallas kernels, fused_device(): pl.pallas_call(functools.partial(gather_kernel, float(frames * tm_count *...  0.79 us

profile of v3, /device:TPU:0, one launch (start us, length us, event | category | flops | bytes accessed | tf_op | source)
XLA Modules:
  0.0 20.4 jit_solution(463726969863099970)
XLA Ops:
  1.3 18.3 %shard_map.86 = (f32[4,64,128]{2,1,0:T(8,128)S(1)}, f32[2,128,128]{2,1,0:T(8,128)S(1)}, f32[16,8,128]{2,1,0:T(8,128)S(1)}) custom-call(f32[2,128,128]{2,1,0:T(8,128)} %phase_hbm.1, f32[2,128,128]{2,1,0:T(8,128)} %direction_hbm.1, s32[1,1]{1,0:T(1,128)} %bitcast.1.tilts, s32[512,128]{1,0:T(8,128)} %mask_hbm.1, s32[512,128]{1,0:T(8,128)} %wind_hbm.1, ...), custom_call_target="tpu_custom_call" | custom-call | tf_op jit(solution)/shard_map/pallas_call | solution.py:811
  19.6 0.8 %shard_map.87 = (f32[2,128,128]{2,1,0:T(8,128)}, f32[1]{0:T(128)}) custom-call(f32[4,64,128]{2,1,0:T(8,128)S(1)} %get-tuple-element.5.grads, f32[2,128,128]{2,1,0:T(8,128)S(1)} %get-tuple-element.6.prior, f32[16,8,128]{2,1,0:T(8,128)S(1)} %get-tuple-element.7.parts), custom_call_target="tpu_custom_call" | custom-call | tf_op jit(solution)/shard_map/pallas_call | solution.py:864

commit v4 on v3

--- a/solution.py
+++ b/solution.py
@@ -303,7 +303,7 @@
     noise,
     table,
     packed_mask,
-    packed_noise,
+    noise_wide,
     turn,
     field,
     operand,
@@ -529,10 +529,16 @@
             ]
         )
 
+    def place(j, row):
+        return j % 2, pl.ds(pl.multiple_of((j // 2) * packed_rows + row, TILE), TILE)
+
     def pack_rows(row):
         packed_mask[pl.ds(row, TILE)] = pack_own(mask, 0, row).astype(jnp.float32)
         for side in range(2):
-            packed_noise[side, pl.ds(row, TILE)] = pack_own(noise, side * pupil, row)
+            wide = widened(pack_own(noise, side * pupil, row))
+            for j in range(pieces):
+                parity, where = place(j, row)
+                noise_wide[side, parity, where] = wide[j]
 
     tiles(packed_rows, pack_rows)
 
@@ -563,9 +569,6 @@
                 turn[1, j, pl.ds(row, TILE), l * rows : (l + 1) * rows] = sine
 
     tiles(packed_rows, turn_rows)
-
-    def place(j, row):
-        return j % 2, pl.ds(pl.multiple_of((j // 2) * packed_rows + row, TILE), TILE)
 
     def put_operand(j, row, l, real, imag):
         for part, value in enumerate((real, imag)):
@@ -673,7 +676,6 @@
 
     def signal_rows(i, power):
         row = pl.multiple_of(i * TILE, TILE)
-        wide_noise = [widened(packed_noise[side, pl.ds(row, TILE)]) for side in range(2)]
         for j in range(pieces):
             parity, where = place(j, row)
             step = dir_wide[parity, where]
@@ -691,8 +693,8 @@
                 odd = odd_l if odd is None else odd + odd_l
             even = 2.0 * over_groups(even)
             odd = over_groups(odd)
-            front = wide_noise[0][j] * (even + odd)
-            back = wide_noise[1][j] * (even - odd)
+            front = noise_wide[0, parity, where] * (even + odd)
+            back = noise_wide[1, parity, where] * (even - odd)
             power = power + front * (even + odd) + back * (even - odd)
             both = front + back
             differ = 0.5 * (front - back)
@@ -724,8 +726,6 @@
             )
         )
         part_copies[-1].start()
-    couple(push)
-
     def grad_rows(row):
         grad = []
         for j in range(pieces):
@@ -742,22 +742,33 @@
             grad.append(2.0 * over_groups(acc))
         send_grad[pl.ds(row, TILE)] = at_lanes(grad)
 
-    tiles(packed_rows, grad_rows)
-
+    side_count, side_rows = mod_count // 2, packed_rows // 2
+    own_side, own_place = mod // side_count, mod % side_count
     grad_copies = []
-    for o in range(1, mod_count):
-        owner = (mod + o) % mod_count
-        grad_copies.append(
-            pltpu.make_async_remote_copy(
-                send_grad.at[pl.ds(pl.multiple_of(owner * sub, sub), sub)],
-                grads.at[mod],
-                grad_send.at[o - 1],
-                grad_recv.at[o - 1],
-                device_id=peer(0, o),
-                device_id_type=pl.DeviceIdType.MESH,
+    for side, first in ((1 - own_side, 0), (own_side, 1)):
+        start = pl.multiple_of(side * side_rows, TILE)
+        for parity in range(2):
+            for block in range(pieces // 2):
+                some = pl.ds(pl.multiple_of(block * packed_rows + start, TILE), side_rows)
+                push[1 - parity, some] = jnp.dot(
+                    table[parity, some], operand[parity], preferred_element_type=jnp.float32
+                )
+        tiles(side_rows, lambda row: grad_rows(pl.multiple_of(start + row, TILE)))
+        for n in range(first, side_count):
+            place_there = (own_place + n) % side_count
+            owner = side * side_count + place_there
+            offset = (owner + mod_count - mod) % mod_count
+            grad_copies.append(
+                pltpu.make_async_remote_copy(
+                    send_grad.at[pl.ds(pl.multiple_of(owner * sub, sub), sub)],
+                    grads.at[mod],
+                    grad_send.at[offset - 1],
+                    grad_recv.at[offset - 1],
+                    device_id={"tm": tm, "mod": owner},
+                    device_id_type=pl.DeviceIdType.MESH,
+                )
             )
-        )
-        grad_copies[-1].start()
+            grad_copies[-1].start()
     grads[mod] = send_grad[my_lines]
 
     for copy in tilt_copies + line_copies[0] + line_copies[1]:
@@ -828,7 +839,7 @@
             pltpu.VMEM(noise_weight.shape[1:], f32),
             pltpu.VMEM((2, half, 3 * half), bf16),
             pltpu.VMEM((packed_rows, rows), f32),
-            pltpu.VMEM((2, packed_rows, rows), f32),
+            pltpu.VMEM((2, 2, half, rows), f32),
             pltpu.VMEM((2, pieces, packed_rows, lanes), f32),
             pltpu.VMEM((2, half, 2 * lanes), f32),
             pltpu.VMEM((2, 3 * half, 2 * lanes), bf16),
@@ -881,6 +892,7 @@
             and rows == 128
             and rows % pieces == 0
             and width % (pieces * TILE) == 0
+            and mod_count % 2 == 0
             and pieces & (pieces - 1) == 0
         )
     run = fused_device if fits else per_device

time: 20.6 us -> 20.6 us (level)
  no operation moved by 1% of the time
where the time goes in v4:
time: 20.6 us; the launch traced here: 20.4 us
  Pallas kernels  19.1 us (93%)
  between operations  1.28 us (6%)
    pallas_call x1, Pallas kernels, fused_device(): pl.pallas_call(functools.partial(fused_kernel, (tm_count, mod_count)), ou...  18.3 us
    pallas_call x1, Pallas kernels, fused_device(): pl.pallas_call(functools.partial(gather_kernel, float(frames * tm_count *...  0.79 us

profile of v4, /device:TPU:0, one launch (start us, length us, event | category | flops | bytes accessed | tf_op | source)
XLA Modules:
  0.0 20.4 jit_solution(8969467381885211392)
XLA Ops:
  1.3 18.3 %shard_map.86 = (f32[4,64,128]{2,1,0:T(8,128)S(1)}, f32[2,128,128]{2,1,0:T(8,128)S(1)}, f32[16,8,128]{2,1,0:T(8,128)S(1)}) custom-call(f32[2,128,128]{2,1,0:T(8,128)} %phase_hbm.1, f32[2,128,128]{2,1,0:T(8,128)} %direction_hbm.1, s32[1,1]{1,0:T(1,128)} %bitcast.1.tilts, s32[512,128]{1,0:T(8,128)} %mask_hbm.1, s32[512,128]{1,0:T(8,128)} %wind_hbm.1, ...), custom_call_target="tpu_custom_call" | custom-call | tf_op jit(solution)/shard_map/pallas_call | solution.py:822
  19.6 0.8 %shard_map.87 = (f32[2,128,128]{2,1,0:T(8,128)}, f32[1]{0:T(128)}) custom-call(f32[4,64,128]{2,1,0:T(8,128)S(1)} %get-tuple-element.5.grads, f32[2,128,128]{2,1,0:T(8,128)S(1)} %get-tuple-element.6.prior, f32[16,8,128]{2,1,0:T(8,128)S(1)} %get-tuple-element.7.parts), custom_call_target="tpu_custom_call" | custom-call | tf_op jit(solution)/shard_map/pallas_call | solution.py:875

commit v5 on v3

--- a/solution.py
+++ b/solution.py
@@ -303,7 +303,7 @@
     noise,
     table,
     packed_mask,
-    packed_noise,
+    noise_wide,
     turn,
     field,
     operand,
@@ -529,10 +529,16 @@
             ]
         )
 
+    def place(j, row):
+        return j % 2, pl.ds(pl.multiple_of((j // 2) * packed_rows + row, TILE), TILE)
+
     def pack_rows(row):
         packed_mask[pl.ds(row, TILE)] = pack_own(mask, 0, row).astype(jnp.float32)
         for side in range(2):
-            packed_noise[side, pl.ds(row, TILE)] = pack_own(noise, side * pupil, row)
+            wide = widened(pack_own(noise, side * pupil, row))
+            for j in range(pieces):
+                parity, where = place(j, row)
+                noise_wide[side, parity, where] = wide[j]
 
     tiles(packed_rows, pack_rows)
 
@@ -563,9 +569,6 @@
                 turn[1, j, pl.ds(row, TILE), l * rows : (l + 1) * rows] = sine
 
     tiles(packed_rows, turn_rows)
-
-    def place(j, row):
-        return j % 2, pl.ds(pl.multiple_of((j // 2) * packed_rows + row, TILE), TILE)
 
     def put_operand(j, row, l, real, imag):
         for part, value in enumerate((real, imag)):
@@ -673,7 +676,6 @@
 
     def signal_rows(i, power):
         row = pl.multiple_of(i * TILE, TILE)
-        wide_noise = [widened(packed_noise[side, pl.ds(row, TILE)]) for side in range(2)]
         for j in range(pieces):
             parity, where = place(j, row)
             step = dir_wide[parity, where]
@@ -691,8 +693,8 @@
                 odd = odd_l if odd is None else odd + odd_l
             even = 2.0 * over_groups(even)
             odd = over_groups(odd)
-            front = wide_noise[0][j] * (even + odd)
-            back = wide_noise[1][j] * (even - odd)
+            front = noise_wide[0, parity, where] * (even + odd)
+            back = noise_wide[1, parity, where] * (even - odd)
             power = power + front * (even + odd) + back * (even - odd)
             both = front + back
             differ = 0.5 * (front - back)
@@ -828,7 +830,7 @@
             pltpu.VMEM(noise_weight.shape[1:], f32),
             pltpu.VMEM((2, half, 3 * half), bf16),
             pltpu.VMEM((packed_rows, rows), f32),
-            pltpu.VMEM((2, packed_rows, rows), f32),
+            pltpu.VMEM((2, 2, half, rows), f32),
             pltpu.VMEM((2, pieces, packed_rows, lanes), f32),
             pltpu.VMEM((2, half, 2 * lanes), f32),
             pltpu.VMEM((2, 3 * half, 2 * lanes), bf16),

time: 20.6 us -> 20.6 us (level)
  no operation moved by 1% of the time
where the time goes in v5:
time: 20.6 us; the launch traced here: 20.4 us
  Pallas kernels  19.1 us (93%)
  between operations  1.28 us (6%)
    pallas_call x1, Pallas kernels, fused_device(): pl.pallas_call(functools.partial(fused_kernel, (tm_count, mod_count)), ou...  18.3 us
    pallas_call x1, Pallas kernels, fused_device(): pl.pallas_call(functools.partial(gather_kernel, float(frames * tm_count *...  0.79 us

profile of v5, /device:TPU:0, one launch (start us, length us, event | category | flops | bytes accessed | tf_op | source)
XLA Modules:
  0.0 20.4 jit_solution(7397703619974764492)
XLA Ops:
  1.3 18.3 %shard_map.86 = (f32[4,64,128]{2,1,0:T(8,128)S(1)}, f32[2,128,128]{2,1,0:T(8,128)S(1)}, f32[16,8,128]{2,1,0:T(8,128)S(1)}) custom-call(f32[2,128,128]{2,1,0:T(8,128)} %phase_hbm.1, f32[2,128,128]{2,1,0:T(8,128)} %direction_hbm.1, s32[1,1]{1,0:T(1,128)} %bitcast.1.tilts, s32[512,128]{1,0:T(8,128)} %mask_hbm.1, s32[512,128]{1,0:T(8,128)} %wind_hbm.1, ...), custom_call_target="tpu_custom_call" | custom-call | tf_op jit(solution)/shard_map/pallas_call | solution.py:813
  19.6 0.8 %shard_map.87 = (f32[2,128,128]{2,1,0:T(8,128)}, f32[1]{0:T(128)}) custom-call(f32[4,64,128]{2,1,0:T(8,128)S(1)} %get-tuple-element.5.grads, f32[2,128,128]{2,1,0:T(8,128)S(1)} %get-tuple-element.6.prior, f32[16,8,128]{2,1,0:T(8,128)S(1)} %get-tuple-element.7.parts), custom_call_target="tpu_custom_call" | custom-call | tf_op jit(solution)/shard_map/pallas_call | solution.py:866
